TPU v7x, 32 devices: a whole 2x2x4 slice. The times are simulated.
32 devices in a mesh: src: 16 (over z, y, x), lev: 2 (over core).
Axes of the slice: x: 2, y: 2, z: 4, core: 2. Of those that a mesh axis runs over, the one named last changes fastest.
Arguments:
- field: bfloat16 [32768, 256], P('src', 'lev'), may hold values from -6 to 6
- grad_coef: float32 [2, 4, 32768], P(None, None, 'src'), may hold values from -6 to 6
- neighbours: int32 [32768, 4], P('src'), may hold values from 0 to 2175, as said below
- level_weight: float32 [8], replicated, may hold values from 0.2 to 2
- src_index: int32 [2048, 64], P('src'), may hold values from 0 to 2047
- tgt_index: int32 [2048, 32], P('src'), may hold values from 0 to 1023
- block_dest: int32 [2048, 1], P('src'), may hold values from 0 to 15; in each aligned block of 128 rows (0 to 127, 128 to 255, ...) at most 16 rows name the same one
- weights: bfloat16 [2048, 6144], P('src'), may hold values from -0.21875 to 0.21875
Outputs:
- remapped: bfloat16 [16384, 256], P('src', 'lev')
- column_total: float32 [32, 16384], P(None, 'src')
Inputs may be any that keep to these rules, and one draw needn't show every extreme that they name: `neighbours`: position 64 + p is the device's own cell p; positions below 64 and from 2112 on are the last and first cells of the devices before and after along the closed curve; a neighbour lies at most 64 cells from the cell. `block_dest`: the 128 blocks of one index of src name one target index at most 16 times.
All inputs are finite; a program needn't handle non-finite values.
Results may differ from a plain program's by a relative error of at most 0.0049.
Values may be sent and summed in bfloat16 or wider, within the bound.
A program may use at most 128 MiB of HBM per device.

v0:
```python
import jax
import jax.numpy as jnp
from jax import lax
from jax.sharding import PartitionSpec as P

FIELDS = 32
HW = 64
SB = 64
TB = 32
T_DEV = 1024


def extended_2(block, sides, width):
    for axis, dim in sides:
        count = lax.axis_size(axis)
        forward = [(i, i + 1) for i in range(count - 1)]
        forward.append((count - 1, 0))
        backward = [(target, source) for source, target in forward]
        low = lax.ppermute(
            lax.slice_in_dim(block, block.shape[dim] - width, None, axis=dim), axis, forward
        )
        high = lax.ppermute(lax.slice_in_dim(block, 0, width, axis=dim), axis, backward)
        block = jnp.concatenate([low, block, high], axis=dim)
    return block


def block_product(block_weights, block_rows):
    block_count = block_rows.shape[0]
    shaped = block_weights.reshape(block_count, 3 * SB, TB)
    return lax.dot_general(
        shaped, block_rows, (((1,), (1,)), ((0,), (0,))), preferred_element_type=jnp.float32
    )


def shards(field, grad_coef, neighbours, level_weight, src_index, tgt_index, block_dest, weights):
    extended = extended_2(field, (("src", 0),), HW)
    own_float = field.astype(jnp.float32)
    differ = extended[neighbours].astype(jnp.float32) - own_float[:, None, :]
    grad_east = jnp.sum(grad_coef[0].T[:, :, None] * differ, axis=1).astype(jnp.bfloat16)
    grad_north = jnp.sum(grad_coef[1].T[:, :, None] * differ, axis=1).astype(jnp.bfloat16)
    recon = jnp.stack([field, grad_east, grad_north])
    columns = field.shape[1]
    block_count = src_index.shape[0]
    block_rows = jnp.transpose(recon[:, src_index], (1, 0, 2, 3)).reshape(
        block_count, 3 * SB, columns
    )
    src_count = lax.axis_size("src")
    capacity = 2 * block_count // src_count
    target_owner = block_dest[:, 0]
    onehot = (target_owner[:, None] == jnp.arange(src_count, dtype=jnp.int32)[None, :]).astype(
        jnp.int32
    )
    before = jnp.cumsum(onehot, axis=0) - onehot
    slot_rank = jnp.sum(before * onehot, axis=1)
    slot_index = target_owner * capacity + slot_rank
    slots = src_count * capacity
    send_cells = jnp.zeros((slots, TB), jnp.int32).at[slot_index].set(tgt_index)
    recv_cells = lax.all_to_all(send_cells, "src", split_axis=0, concat_axis=0, tiled=True)
    partial_value = block_product(weights, block_rows)
    send_partial = jnp.zeros((slots, TB, columns), jnp.float32).at[slot_index].set(partial_value)
    received = lax.all_to_all(send_partial, "src", split_axis=0, concat_axis=0, tiled=True)
    total = (
        jnp.zeros((T_DEV, columns), jnp.float32)
        .at[recv_cells.reshape(-1)]
        .add(received.reshape(-1, columns))
    )
    remapped = total.astype(jnp.bfloat16)
    level_count = columns // FIELDS
    level_share = lax.dynamic_slice_in_dim(
        level_weight, lax.axis_index("lev") * level_count, level_count
    )
    local_sum = jnp.einsum(
        "tlf,l->ft",
        total.reshape(T_DEV, level_count, FIELDS),
        level_share,
        precision=lax.Precision.HIGHEST,
    )
    column_total = lax.psum(local_sum, "lev")
    return (remapped, column_total)


def solution(mesh):
    placed = (
        P("src", "lev"),
        P(None, None, "src"),
        P("src", None),
        P(),
        P("src", None),
        P("src", None),
        P("src", None),
        P("src", None),
    )
    return jax.shard_map(
        shards,
        mesh=mesh,
        in_specs=placed,
        out_specs=(P("src", "lev"), P(None, "src")),
        check_vma=False,
    )
```

profile of v0, /device:TPU:0, one launch (start us, length us, event | category | flops | bytes accessed | tf_op | source)
XLA Modules:
  0.0 406.4 jit_solution(9051789890176872774)
XLA Ops:
  7.2 0.8 fusion.14
  8.0 3.0 collective-permute-start
  11.0 4.0 collective-permute-start.1
  15.9 0.8 select_reduce_fusion
  17.4 0.8 copy.23
  18.2 0.9 scatter_custom_fusion
  19.8 3.5 all-to-all-start
  23.3 0.8 compare_select_fusion.2
  25.1 0.8 slice_bitcast_fusion
  26.9 2.1 convert_element_type.40
  29.0 1.4 copy.24
  30.4 1.4 copy.26
  31.7 8.9 %copy.27 = bf16[1,2048,128]{2,0,1:T(2,128)(2,1)} copy(bf16[1,2048,128]{2,1,0:T(8,128)(2,1)S(1)} %bitcast.47) | data formatting | bytes 1048576 | tf_op jit(solution)/shard_map/stack | solution.py:41
  40.6 1.9 copy.32
  42.6 3.4 copy.33
  46.0 24.0 %gather_fusion = bf16[8192,128]{1,0:T(8,128)(2,1)S(1)} fusion(bf16[2176,128]{1,0:T(8,128)(2,1)S(1)} %pad_maximum_fusion.1, s32[8192]{0:T(1024)S(1)} %broadcast_clamp_fusion.1), kind=kCustom, calls=%fused_computation | custom fusion | bytes 4227072 | tf_op jit(solution)/shard_map/gather | solution.py:38
  70.0 15.1 %fusion.2 = (bf16[2048,128]{1,0:T(8,128)(2,1)S(1)}, bf16[2048,128]{1,0:T(8,128)(2,1)S(1)}) fusion(bf16[2048,4,128]{2,1,0:T(4,128)(2,1)S(1)} %bitcast.45, f32[2048,128]{1,0:T(8,128)} %convert_element_type.40, f32[2048,4]{1,0:T(8,128)} %copy.24, f32[2048,4]{1,0:T(8,128)} %copy.26), kind=kLoop, calls=%fused_computation.8 | loop fusion | flops 5767168 | bytes 4259840 | tf_op jit(solution)/shard_map/reduce_sum | solution.py:39
  85.1 8.3 %copy.28 = bf16[1,2048,128]{2,0,1:T(2,128)(2,1)S(1)} copy(bf16[1,2048,128]{2,1,0:T(8,128)(2,1)S(1)} %bitcast.50) | data formatting | bytes 1048576 | tf_op jit(solution)/shard_map/convert_element_type | solution.py:39
  93.4 8.1 %copy.29 = bf16[1,2048,128]{2,0,1:T(2,128)(2,1)S(1)} copy(bf16[1,2048,128]{2,1,0:T(8,128)(2,1)S(1)} %bitcast.49) | data formatting | bytes 1048576 | tf_op jit(solution)/shard_map/convert_element_type | solution.py:40
  101.6 3.6 pad_maximum_fusion
  105.1 56.5 %gather_fusion.1 = bf16[8192,3,128]{2,1,0:T(4,128)(2,1)} fusion(bf16[3,2048,128]{2,0,1:T(4,128)(2,1)S(1)} %pad_maximum_fusion, s32[8192]{0:T(1024)S(1)} %broadcast_clamp_fusion), kind=kCustom, calls=%fused_computation.1 | custom fusion | bytes 12615680 | tf_op jit(solution)/shard_map/gather | solution.py:44
  161.6 5.5 %copy.31 = bf16[128,3,64,128]{3,2,1,0:T(8,128)(2,1)S(1)} copy(bf16[128,3,64,128]{3,1,2,0:T(4,128)(2,1)} %bitcast.43) | data formatting | bytes 12582912 | tf_op jit(solution)/shard_map/transpose | solution.py:44
  167.1 2.4 convolution_bitcast_fusion
  169.5 2.5 broadcast_in_dim.24
  172.0 15.7 %scatter_fusion = f32[256,32,128]{2,1,0:T(8,128)} fusion(f32[256,32,128]{2,1,0:T(8,128)} %broadcast_in_dim.24, s32[128]{0:T(128)S(1)} %fusion.11, f32[128,32,128]{2,1,0:T(8,128)S(1)} %convolution_bitcast_fusion), kind=kCustom, calls=%fused_computation.3 | custom fusion | bytes 6291968 | tf_op jit(solution)/shard_map/scatter | solution.py:60
  187.7 6.9 %all-to-all-start.1 = ((f32[256,32,128]{2,1,0:T(8,128)}), f32[256,32,128]{2,1,0:T(8,128)}, u32[]{:S(2)}, u32[]{:S(2)}) async-start(f32[256,32,128]{2,1,0:T(8,128)} %scatter_fusion), calls=%async_computation.1 | async-start | bytes 8388608 | tf_op jit(solution)/shard_map/all_to_all | solution.py:61
  196.2 77.1 %all-to-all-done.1 = f32[256,32,128]{2,1,0:T(8,128)} async-done(((f32[256,32,128]{2,1,0:T(8,128)}), f32[256,32,128]{2,1,0:T(8,128)}, u32[]{:S(2)}, u32[]{:S(2)}) %all-to-all-start.1) | async-done | bytes 4194336 | tf_op jit(solution)/shard_map/all_to_all | solution.py:61
  273.3 53.3 %scatter_custom_fusion.2 = f32[1024,128]{1,0:T(8,128)S(1)} fusion(s32[8192]{0:T(1024)S(1)} %bitcast.53, f32[8192,128]{1,0:T(8,128)} %bitcast.18, f32[]{:T(128)} %constant.10.clone.1), kind=kCustom, calls=%fused_computation.17 | custom fusion | flops 1048576 | bytes 524800 | tf_op jit(solution)/shard_map/scatter-add | solution.py:65
  326.8 29.1 %fusion.4 = f32[1,1024,32]{0,1,2:T(8,128)} fusion(f32[1024,4,32]{0,2,1:T(8,128)S(1)} %bitcast.48, f32[8]{0:T(128)S(1)} %copy-done, s32[]{:T(128)S(6)} %select_n.28), kind=kOutput, calls=%fused_computation.13 | convolution fusion | flops 1572864 | bytes 655396 | tf_op jit(solution)/shard_map/tlf,l->ft/dot_general | solution.py:72
  356.0 10.6 %copy.36 = f32[1,1024,32]{1,2,0:T(8,128)} copy(f32[1,1024,32]{0,1,2:T(8,128)} %fusion.4) | data formatting | bytes 262144 | tf_op jit(solution)/shard_map/tlf,l->ft/dot_general | solution.py:72
  367.3 30.7 %all-reduce.2.cloned.1.call-done = f32[32,1024]{1,0:T(8,128)} async-done(((f32[32,1024]{1,0:T(8,128)}), f32[32,1024]{1,0:T(8,128)}) %all-reduce.2.cloned.1.call-update) | async-done | bytes 131088 | tf_op jit(solution)/shard_map/psum | solution.py:78
  398.0 1.6 copy.41
  (32 shorter events, 6.8 us)
Async XLA Ops:
  7.2 319.6 %copy-start = (f32[8]{0:T(128)S(1)}, f32[8]{0:T(128)}, u32[]{:S(2)}) copy-start(f32[8]{0:T(128)} %param.11) | copy-start | bytes 100
  7.2 24.6 %copy-start.2 = (bf16[2048,128]{1,0:T(8,128)(2,1)S(1)}, bf16[2048,128]{1,0:T(8,128)(2,1)}, u32[]{:S(2)}) copy-start(bf16[2048,128]{1,0:T(8,128)(2,1)} %param.8) | copy-start | bytes 1572868
  8.0 37.9 %collective-permute-start = (bf16[64,128]{1,0:T(8,128)(2,1)S(1)}, bf16[64,128]{1,0:T(8,128)(2,1)S(1)}, u32[]{:S(2)}, u32[]{:S(2)}) collective-permute-start(bf16[64,128]{1,0:T(8,128)(2,1)S(1)} %get-tuple-element.4), channel_id=1, source_target_pairs={{0,2},{2,4},{4,6},{6,8},{8,10},{10,12},{12,14},{14,16},{16,18},{18... | collective-permute-start | bytes 49160 | tf_op jit(solution)/shard_map/ppermute | solution.py:19
  11.0 35.0 %collective-permute-start.1 = (bf16[64,128]{1,0:T(8,128)(2,1)S(1)}, bf16[64,128]{1,0:T(8,128)(2,1)S(1)}, u32[]{:S(2)}, u32[]{:S(2)}) collective-permute-start(bf16[64,128]{1,0:T(8,128)(2,1)S(1)} %get-tuple-element.5), channel_id=1, source_target_pairs={{2,0},{4,2},{6,4},{8,6},{10,8},{12,10},{14,12},{16,14},{18,16},{20... | collective-permute-start | bytes 49160 | tf_op jit(solution)/shard_map/ppermute | solution.py:22
  19.8 167.9 %all-to-all-start = ((s32[16,1,512]{2,1,0:T(1,128)}), s32[16,1,512]{2,1,0:T(1,128)S(1)}, u32[]{:S(2)}, u32[]{:S(2)}) async-start(s32[16,1,512]{2,1,0:T(1,128)} %reshape.126), calls=%async_computation | async-start | bytes 65536 | tf_op jit(solution)/shard_map/all_to_all | solution.py:58
  70.0 31.5 %copy-start.3 = (bf16[1,2048,128]{2,0,1:T(2,128)(2,1)S(1)}, bf16[1,2048,128]{2,0,1:T(2,128)(2,1)}, u32[]{:S(2)}) copy-start(bf16[1,2048,128]{2,0,1:T(2,128)(2,1)} %copy.27) | copy-start | bytes 1572868
  161.6 5.5 %copy-start.1 = (bf16[128,192,32]{1,2,0:T(8,128)(2,1)S(1)}, bf16[128,192,32]{1,2,0:T(8,128)(2,1)}, u32[]{:S(2)}) copy-start(bf16[128,192,32]{1,2,0:T(8,128)(2,1)} %copy.33) | copy-start | bytes 4718596
  187.7 85.6 %all-to-all-start.1 = ((f32[256,32,128]{2,1,0:T(8,128)}), f32[256,32,128]{2,1,0:T(8,128)}, u32[]{:S(2)}, u32[]{:S(2)}) async-start(f32[256,32,128]{2,1,0:T(8,128)} %scatter_fusion), calls=%async_computation.1 | async-start | bytes 8388608 | tf_op jit(solution)/shard_map/all_to_all | solution.py:61
  194.7 203.3 %all-reduce.2.cloned.1.call-start = ((), (), s32[]{:S(2)}) async-start(), calls=%async_computation.2 | async-start | bytes 262144 | tf_op jit(solution)/shard_map/psum | solution.py:78
Sparse Core Ops, SparseCore 0:
  366.7 31.2 all-reduce.1
where the time goes:
time: 408 us; the launch traced here: 406 us
  local copies, waits for them, and re-layouts  156 us (38%)
  waiting for transfers between devices  108 us (26%)
  other arithmetic  79.5 us (19%)
  matrix products  31.6 us (8%)
  starting transfers between devices  17.4 us (4%)
  between operations  14.3 us (4%)
    all_to_all x1, waiting for transfers between devices, shards(): lax.all_to_all(send_partial, 'src', split_axis=0, concat_axis=0, tiled=True)  77.1 us
    gather x1, local copies, waits for them, and re-layouts, shards(): recon[:, src_index]  56.5 us
    scatter-add x1, other arithmetic, shards(): total = jnp.zeros((T_DEV, columns), jnp.float32).at[recv_cells.reshape(-1...  53.3 us
    psum x1, waiting for transfers between devices, shards(): column_total = lax.psum(local_sum, 'lev')  30.7 us
    dot_general x1, matrix products, shards(): jnp.einsum('tlf,l->ft', total.reshape(T_DEV, level_count, FIELDS), level_...  29.1 us
    gather x1, local copies, waits for them, and re-layouts, shards(): differ = extended[neighbours].astype(jnp.float32) - own_float[:, None, :]  24 us
    scatter x1, local copies, waits for them, and re-layouts, shards(): jnp.zeros((slots, TB, columns), jnp.float32).at[slot_index]  15.7 us
    reduce_sum x1, other arithmetic, shards(): jnp.sum(grad_coef[0].T[:, :, None] * differ, axis=1).astype(jnp.bfloat16)  15.1 us
  transfers between devices with their start and end apart: 5, of which 2 were waited for; matrix products, arithmetic and copies ran while one was open for 42% of the time, Pallas kernels for 0%

commit v1 on v0

--- a/solution.py
+++ b/solution.py
@@ -33,6 +33,10 @@
 
 
 def shards(field, grad_coef, neighbours, level_weight, src_index, tgt_index, block_dest, weights):
+
+    def move_strings_now(vector):
+        return jnp.sum(lax.all_gather(vector, "lev"), 0)
+
     extended = extended_2(field, (("src", 0),), HW)
     own_float = field.astype(jnp.float32)
     differ = extended[neighbours].astype(jnp.float32) - own_float[:, None, :]
@@ -75,7 +79,7 @@
         level_share,
         precision=lax.Precision.HIGHEST,
     )
-    column_total = lax.psum(local_sum, "lev")
+    column_total = move_strings_now(local_sum)
     return (remapped, column_total)
 
 

time: 408 us -> 377 us (0.924)
  the two profiles are of different devices: /device:TPU:0 before, /device:TPU:17 now
where the time goes in v1:
time: 377 us; the launch traced here: 376 us
  local copies, waits for them, and re-layouts  154 us (41%)
  waiting for transfers between devices  89.6 us (24%)
  other arithmetic  81.2 us (22%)
  matrix products  31.3 us (8%)
  starting transfers between devices  15 us (4%)
  blocking collectives  4 us (1%)
    all_to_all x1, waiting for transfers between devices, shards(): lax.all_to_all(send_partial, 'src', split_axis=0, concat_axis=0, tiled=True)  89.6 us
    gather x1, local copies, waits for them, and re-layouts, shards(): recon[:, src_index]  56.5 us
    scatter-add x1, other arithmetic, shards(): total = jnp.zeros((T_DEV, columns), jnp.float32).at[recv_cells.reshape(-1...  54.4 us
    dot_general x1, matrix products, shards(): jnp.einsum('tlf,l->ft', total.reshape(T_DEV, level_count, FIELDS), level_...  28.9 us
    gather x1, local copies, waits for them, and re-layouts, shards(): differ = extended[neighbours].astype(jnp.float32) - own_float[:, None, :]  24 us
    scatter x1, local copies, waits for them, and re-layouts, shards(): jnp.zeros((slots, TB, columns), jnp.float32).at[slot_index]  15.7 us
    reduce_sum x1, other arithmetic, shards(): jnp.sum(grad_coef[0].T[:, :, None] * differ, axis=1).astype(jnp.bfloat16)  15.1 us
    dot_general x1, local copies, waits for them, and re-layouts, shards(): jnp.einsum('tlf,l->ft', total.reshape(T_DEV, level_count, FIELDS), level_...  9.95 us
  transfers between devices with their start and end apart: 4, of which 1 were waited for; matrix products, arithmetic and copies ran while one was open for 45% of the time, Pallas kernels for 0%

profile of v1, /device:TPU:17, one launch (start us, length us, event | category | flops | bytes accessed | tf_op | source)
XLA Modules:
  0.0 375.6 jit_solution(5238388410790337901)
XLA Ops:
  0.7 0.8 fusion.14
  1.5 1.2 collective-permute-start
  2.7 2.1 collective-permute-start.1
  5.6 0.8 select_reduce_fusion
  7.1 0.8 copy.23
  7.9 0.9 scatter_custom_fusion
  9.6 5.3 %all-to-all-start = ((s32[16,1,512]{2,1,0:T(1,128)}), s32[16,1,512]{2,1,0:T(1,128)S(1)}, u32[]{:S(2)}, u32[]{:S(2)}) async-start(s32[16,1,512]{2,1,0:T(1,128)} %reshape.127), calls=%async_computation | async-start | bytes 65536 | tf_op jit(solution)/shard_map/all_to_all | solution.py:62
  14.9 0.8 compare_select_fusion.2
  16.7 0.8 slice_bitcast_fusion
  17.5 0.8 compare_select_fusion.1
  18.5 2.1 convert_element_type.40
  20.6 1.4 copy.24
  22.0 1.4 copy.26
  23.3 8.9 %copy.27 = bf16[1,2048,128]{2,0,1:T(2,128)(2,1)} copy(bf16[1,2048,128]{2,1,0:T(8,128)(2,1)S(1)} %bitcast.48) | data formatting | bytes 1048576 | tf_op jit(solution)/shard_map/stack | solution.py:45
  32.2 1.9 copy.32
  34.1 3.4 copy.33
  37.6 24.0 %gather_fusion = bf16[8192,128]{1,0:T(8,128)(2,1)S(1)} fusion(bf16[2176,128]{1,0:T(8,128)(2,1)S(1)} %pad_maximum_fusion.1, s32[8192]{0:T(1024)S(1)} %broadcast_clamp_fusion.1), kind=kCustom, calls=%fused_computation | custom fusion | bytes 4227072 | tf_op jit(solution)/shard_map/gather | solution.py:42
  61.6 15.1 %fusion.2 = (bf16[2048,128]{1,0:T(8,128)(2,1)S(1)}, bf16[2048,128]{1,0:T(8,128)(2,1)S(1)}) fusion(bf16[2048,4,128]{2,1,0:T(4,128)(2,1)S(1)} %bitcast.46, f32[2048,128]{1,0:T(8,128)} %convert_element_type.40, f32[2048,4]{1,0:T(8,128)} %copy.24, f32[2048,4]{1,0:T(8,128)} %copy.26), kind=kLoop, calls=%fused_computation.8 | loop fusion | flops 5767168 | bytes 4259840 | tf_op jit(solution)/shard_map/reduce_sum | solution.py:43
  76.7 8.3 %copy.28 = bf16[1,2048,128]{2,0,1:T(2,128)(2,1)S(1)} copy(bf16[1,2048,128]{2,1,0:T(8,128)(2,1)S(1)} %bitcast.51) | data formatting | bytes 1048576 | tf_op jit(solution)/shard_map/convert_element_type | solution.py:43
  85.0 8.1 %copy.29 = bf16[1,2048,128]{2,0,1:T(2,128)(2,1)S(1)} copy(bf16[1,2048,128]{2,1,0:T(8,128)(2,1)S(1)} %bitcast.50) | data formatting | bytes 1048576 | tf_op jit(solution)/shard_map/convert_element_type | solution.py:44
  93.2 3.6 pad_maximum_fusion
  96.7 56.5 %gather_fusion.1 = bf16[8192,3,128]{2,1,0:T(4,128)(2,1)} fusion(bf16[3,2048,128]{2,0,1:T(4,128)(2,1)S(1)} %pad_maximum_fusion, s32[8192]{0:T(1024)S(1)} %broadcast_clamp_fusion), kind=kCustom, calls=%fused_computation.1 | custom fusion | bytes 12615680 | tf_op jit(solution)/shard_map/gather | solution.py:48
  153.2 5.5 %copy.31 = bf16[128,3,64,128]{3,2,1,0:T(8,128)(2,1)S(1)} copy(bf16[128,3,64,128]{3,1,2,0:T(4,128)(2,1)} %bitcast.44) | data formatting | bytes 12582912 | tf_op jit(solution)/shard_map/transpose | solution.py:48
  158.7 2.4 convolution_bitcast_fusion
  161.1 2.5 broadcast_in_dim.24
  163.6 15.7 %scatter_fusion = f32[256,32,128]{2,1,0:T(8,128)} fusion(f32[256,32,128]{2,1,0:T(8,128)} %broadcast_in_dim.24, s32[128]{0:T(128)S(1)} %fusion.11, f32[128,32,128]{2,1,0:T(8,128)S(1)} %convolution_bitcast_fusion), kind=kCustom, calls=%fused_computation.3 | custom fusion | bytes 6291968 | tf_op jit(solution)/shard_map/scatter | solution.py:64
  179.3 6.4 %all-to-all-start.1 = ((f32[256,32,128]{2,1,0:T(8,128)}), f32[256,32,128]{2,1,0:T(8,128)}, u32[]{:S(2)}, u32[]{:S(2)}) async-start(f32[256,32,128]{2,1,0:T(8,128)} %scatter_fusion), calls=%async_computation.1 | async-start | bytes 8388608 | tf_op jit(solution)/shard_map/all_to_all | solution.py:65
  187.2 89.6 %all-to-all-done.1 = f32[256,32,128]{2,1,0:T(8,128)} async-done(((f32[256,32,128]{2,1,0:T(8,128)}), f32[256,32,128]{2,1,0:T(8,128)}, u32[]{:S(2)}, u32[]{:S(2)}) %all-to-all-start.1) | async-done | bytes 4194336 | tf_op jit(solution)/shard_map/all_to_all | solution.py:65
  276.8 54.4 %scatter_custom_fusion.2 = f32[1024,128]{1,0:T(8,128)S(1)} fusion(s32[8192]{0:T(1024)S(1)} %bitcast.55, f32[8192,128]{1,0:T(8,128)} %bitcast.18, f32[]{:T(128)} %constant.10.clone.1), kind=kCustom, calls=%fused_computation.17 | custom fusion | flops 1048576 | bytes 524800 | tf_op jit(solution)/shard_map/scatter-add | solution.py:69
  332.1 28.9 %fusion.4 = f32[1,1024,32]{0,1,2:T(8,128)} fusion(f32[1024,4,32]{0,2,1:T(8,128)S(1)} %bitcast.49, f32[8]{0:T(128)S(1)} %copy-done, s32[]{:T(128)S(6)} %select_n.28), kind=kOutput, calls=%fused_computation.13 | convolution fusion | flops 1572864 | bytes 655396 | tf_op jit(solution)/shard_map/tlf,l->ft/dot_general | solution.py:76
  361.0 10.0 %copy.36 = f32[1,1024,32]{1,2,0:T(8,128)S(1)} copy(f32[1,1024,32]{0,1,2:T(8,128)} %fusion.4) | data formatting | bytes 262144 | tf_op jit(solution)/shard_map/tlf,l->ft/dot_general | solution.py:76
  370.9 4.0 %all-gather = f32[64,1024]{1,0:T(8,128)S(1)} all-gather(f32[32,1024]{1,0:T(8,128)S(1)} %bitcast.53), channel_id=2, replica_groups=mesh['src'=16,'lev'=2] {'lev'}, dimensions={0}, use_global_device_ids=true | all-gather | bytes 393216 | tf_op jit(solution)/shard_map/all_gather | solution.py:38
  (30 shorter events, 6.6 us)
Async XLA Ops:
  0.6 331.5 %copy-start = (f32[8]{0:T(128)S(1)}, f32[8]{0:T(128)}, u32[]{:S(2)}) copy-start(f32[8]{0:T(128)} %param.11) | copy-start | bytes 100
  0.6 22.7 %copy-start.2 = (bf16[2048,128]{1,0:T(8,128)(2,1)S(1)}, bf16[2048,128]{1,0:T(8,128)(2,1)}, u32[]{:S(2)}) copy-start(bf16[2048,128]{1,0:T(8,128)(2,1)} %param.8) | copy-start | bytes 1572868
  1.5 36.1 %collective-permute-start = (bf16[64,128]{1,0:T(8,128)(2,1)S(1)}, bf16[64,128]{1,0:T(8,128)(2,1)S(1)}, u32[]{:S(2)}, u32[]{:S(2)}) collective-permute-start(bf16[64,128]{1,0:T(8,128)(2,1)S(1)} %get-tuple-element.4), channel_id=1, source_target_pairs={{0,2},{2,4},{4,6},{6,8},{8,10},{10,12},{12,14},{14,16},{16,18},{18... | collective-permute-start | bytes 49160 | tf_op jit(solution)/shard_map/ppermute | solution.py:19
  2.7 34.9 %collective-permute-start.1 = (bf16[64,128]{1,0:T(8,128)(2,1)S(1)}, bf16[64,128]{1,0:T(8,128)(2,1)S(1)}, u32[]{:S(2)}, u32[]{:S(2)}) collective-permute-start(bf16[64,128]{1,0:T(8,128)(2,1)S(1)} %get-tuple-element.5), channel_id=1, source_target_pairs={{2,0},{4,2},{6,4},{8,6},{10,8},{12,10},{14,12},{16,14},{18,16},{20... | collective-permute-start | bytes 49160 | tf_op jit(solution)/shard_map/ppermute | solution.py:22
  9.6 169.7 %all-to-all-start = ((s32[16,1,512]{2,1,0:T(1,128)}), s32[16,1,512]{2,1,0:T(1,128)S(1)}, u32[]{:S(2)}, u32[]{:S(2)}) async-start(s32[16,1,512]{2,1,0:T(1,128)} %reshape.127), calls=%async_computation | async-start | bytes 65536 | tf_op jit(solution)/shard_map/all_to_all | solution.py:62
  61.6 31.5 %copy-start.3 = (bf16[1,2048,128]{2,0,1:T(2,128)(2,1)S(1)}, bf16[1,2048,128]{2,0,1:T(2,128)(2,1)}, u32[]{:S(2)}) copy-start(bf16[1,2048,128]{2,0,1:T(2,128)(2,1)} %copy.27) | copy-start | bytes 1572868
  153.2 5.5 %copy-start.1 = (bf16[128,192,32]{1,2,0:T(8,128)(2,1)S(1)}, bf16[128,192,32]{1,2,0:T(8,128)(2,1)}, u32[]{:S(2)}) copy-start(bf16[128,192,32]{1,2,0:T(8,128)(2,1)} %copy.33) | copy-start | bytes 4718596
  179.3 97.5 %all-to-all-start.1 = ((f32[256,32,128]{2,1,0:T(8,128)}), f32[256,32,128]{2,1,0:T(8,128)}, u32[]{:S(2)}, u32[]{:S(2)}) async-start(f32[256,32,128]{2,1,0:T(8,128)} %scatter_fusion), calls=%async_computation.1 | async-start | bytes 8388608 | tf_op jit(solution)/shard_map/all_to_all | solution.py:65
